TPU v7x, 32 devices: a whole 2x2x4 slice. The times are simulated.
32 devices in a mesh: chan: 16 (over z, x, core), pix: 2 (over y).
Axes of the slice: x: 2, y: 2, z: 4, core: 2. Of those that a mesh axis runs over, the one named last changes fastest.
Arguments:
- cube: float32 [512, 16384], P('pix', 'chan'), as said below
- windows: int32 [8], replicated, may hold values from 1 to 1024, as said below
- mask: int32 [16384], replicated, may hold values from 0 to 1, as said below
Outputs:
- subtracted: float32 [512, 16384], P('pix', 'chan')
Inputs may be any that keep to these rules, and one draw needn't show every extreme that they name: windows[0] is 1024 and windows[7] is 1; for 0 < k < 7, windows[k] is at most 1024 halved k times (rounded down) and more than three quarters of that, but 1 or more. `mask`: zero on 8 disjoint ranges of 256 to 512 channels each, one elsewhere; the k-th range lies inside channels k * 2048 to (k + 1) * 2048 - 1, at least 512 channels from that slot's edges, and at least 1024 channels from either end of the band. `cube`: each spectrum is a smooth continuum of low order plus noise whose level varies from channel to channel.
All inputs are finite; a program needn't handle non-finite values.
Results may differ from a plain program's by a relative error of at most 0.00021.
Values sent between devices are 32-bit elements; how exact they have to be, the bound alone decides.
A program may use at most 64 MiB of HBM per device.

v0:
```python
import functools
import math

import jax
import jax.numpy as jnp
import numpy as np
from jax import lax
from jax.experimental import pallas as pl
from jax.experimental.pallas import tpu as pltpu
from jax.sharding import PartitionSpec as P

TERMS = 16
PASSES = 8
WMAX = 1024
HALO = 2 * WMAX
LANES = 128
BLOCK = 16
CHUNKS = 4
SPLIT = 2
TAIL = True
MESH = pl.DeviceIdType.MESH
F32 = jnp.float32
BF16 = jnp.bfloat16


def chunk_spans(rows):
    part = rows // CHUNKS
    sizes = [part] * CHUNKS
    if TAIL and part >= 16:
        sizes[-1:] = [part // 2, part // 2]
    starts = [sum(sizes[:i]) for i in range(len(sizes))]
    return list(zip(starts, sizes))


def linearization():
    def a(r):
        return math.comb(2 * r, r) / 2.0**r

    out = np.zeros((2 * TERMS - 1, TERMS, TERMS))
    for n in range(TERMS):
        for m in range(TERMS):
            for r in range(min(n, m) + 1):
                k = n + m - 2 * r
                out[k, n, m] = (
                    a(r) * a(n - r) * a(m - r) / a(n + m - r)
                    * (2 * k + 1) / (2 * n + 2 * m - 2 * r + 1)
                )
    return out.astype(np.float32)


def next_legendre(order, xvals, here, before):
    return ((2.0 * order + 1.0) * xvals * here - order * before) * (1.0 / (order + 1.0))


def split3(v):
    hi = v.astype(BF16)
    rest = v - hi.astype(F32)
    mid = rest.astype(BF16)
    lo = (rest - mid.astype(F32)).astype(BF16)
    return hi, mid, lo


def kernel(
    n_chan, group, total,
    windows_hbm, cube, mask_sq_hbm, mask_row_hbm, lin_hbm,
    left_out, right_hbm,
    windows, right_out, mask_sq, mask_row, lin, raw, ping, pong, fit, table, w3, sums,
    load_sem, right_sem, token, own_sem, send_sem, hop_sem, recv_sem, up_sem, down_sem, sum_send, sum_recv,
):
    pix, ch = cube.shape
    rows = raw.shape[0]
    slab_ch = group * ch
    tiles = slab_ch // LANES
    slabs = n_chan // group
    spans = chunk_spans(rows)
    me = lax.axis_index("chan")
    slab = me // group
    g = lax.rem(me, group)
    own_col = pl.multiple_of(HALO + g * ch, LANES)

    def peer(b):
        return {"chan": slab * group + b}

    own_rows = pl.multiple_of(g * rows, 8)
    barrier = pltpu.get_barrier_semaphore()

    def greet(device):
        pl.semaphore_signal(
            barrier, inc=1, device_id={"chan": device}, device_id_type=MESH
        )

    for k in range(1, group):
        greet(slab * group + lax.rem(g + k, group))

    @pl.when(slab > 0)
    def _():
        greet(me - group)

    @pl.when(slab < slabs - 1)
    def _():
        greet(me + group)

    loads = [
        pltpu.make_async_copy(mask_sq_hbm, mask_sq, load_sem.at[0]),
        pltpu.make_async_copy(mask_row_hbm, mask_row, load_sem.at[1]),
        pltpu.make_async_copy(lin_hbm, lin, load_sem.at[2]),
        pltpu.make_async_copy(windows_hbm, windows, load_sem.at[3]),
    ]
    own = pltpu.make_async_copy(
        cube.at[pl.ds(own_rows, rows), :], raw.at[:, pl.ds(own_col, ch)], own_sem
    )
    for copy in loads:
        copy.start()
    own.start()

    @pl.when(slab == 0)
    def _():
        raw[:, 0:HALO] = jnp.full((rows, HALO), jnp.inf, F32)

    @pl.when(slab == slabs - 1)
    def _():
        raw[:, HALO + slab_ch :] = jnp.full((rows, HALO), jnp.inf, F32)

    near = group - 1 + jnp.where(slab > 0, 1, 0) + jnp.where(slab < slabs - 1, 1, 0)
    pl.semaphore_wait(barrier, near)

    points = min(slabs, 3)

    def relay(point):
        for up in (True, False):
            place = slab if up else slabs - 1 - slab
            sem = token.at[0 if up else 1]
            to = me + group if up else me - group
            turn = (place == point) if point < points - 1 else (place >= point)

            @pl.when(turn)
            def _():
                if point > 0:
                    pl.semaphore_wait(sem, 1)

                @pl.when(place < slabs - 1)
                def _():
                    pl.semaphore_signal(
                        sem, inc=1, device_id={"chan": to}, device_id_type=MESH
                    )

    def chunk(c):
        return pl.ds(*spans[c])

    def slab_send(c, b):
        return pltpu.make_async_remote_copy(
            src_ref=cube.at[pl.ds(b * rows + spans[c][0], spans[c][1]), :],
            dst_ref=raw.at[chunk(c), pl.ds(own_col, ch)],
            send_sem=send_sem, recv_sem=recv_sem.at[c, g],
            device_id=peer(b), device_id_type=MESH,
        )

    def slab_recv(c, b):
        return pltpu.make_async_remote_copy(
            src_ref=cube.at[chunk(c), :],
            dst_ref=raw.at[chunk(c), pl.ds(HALO + b * ch, ch)],
            send_sem=send_sem, recv_sem=recv_sem.at[c, b],
            device_id=peer(b), device_id_type=MESH,
        )

    def hop(c, b, up, from_own):
        if up:
            col = b * ch - (slab_ch - HALO)
            sem, to = up_sem.at[c], me + group
        else:
            col = HALO + slab_ch + b * ch
            sem, to = down_sem.at[c], me - group
        if from_own:
            src = cube.at[pl.ds(pl.multiple_of(own_rows + spans[c][0], 8), spans[c][1]), :]
        else:
            src = raw.at[chunk(c), pl.ds(HALO + b * ch, ch)]
        return pltpu.make_async_remote_copy(
            src_ref=src, dst_ref=raw.at[chunk(c), pl.ds(col, ch)],
            send_sem=hop_sem.at[0 if up else 1], recv_sem=sem,
            device_id={"chan": to}, device_id_type=MESH,
        )

    def goes_up(b):
        return b * ch >= slab_ch - HALO

    def goes_down(b):
        return b * ch < HALO

    def own_hops(c):
        for b in range(group):
            if goes_up(b):
                @pl.when((g == b) & (slab < slabs - 1))
                def _():
                    hop(c, b, True, True).start()
            if goes_down(b):
                @pl.when((g == b) & (slab > 0))
                def _():
                    hop(c, b, False, True).start()

    def forward(c):
        for b in range(group):
            @pl.when(g != b)
            def _():
                slab_recv(c, b).wait_recv()
                if goes_up(b):
                    @pl.when(slab < slabs - 1)
                    def _():
                        hop(c, b, True, False).start()
                if goes_down(b):
                    @pl.when(slab > 0)
                    def _():
                        hop(c, b, False, False).start()

    def halo_wait(c):
        def arrived(col, sem):
            return pltpu.make_async_remote_copy(
                src_ref=raw.at[chunk(c), pl.ds(col, HALO)],
                dst_ref=raw.at[chunk(c), pl.ds(col, HALO)],
                send_sem=hop_sem.at[0], recv_sem=sem,
                device_id={"chan": me}, device_id_type=MESH,
            )

        @pl.when(slab > 0)
        def _():
            arrived(0, up_sem.at[c]).wait_recv()

        @pl.when(slab < slabs - 1)
        def _():
            arrived(HALO + slab_ch, down_sem.at[c]).wait_recv()

    for c in range(len(spans)):
        for b in range(group):
            @pl.when(g != b)
            def _():
                slab_send(c, b).start()
        own_hops(c)
    relay(0)
    for copy in loads:
        copy.wait()

    shape = mask_sq.shape
    index = lax.broadcasted_iota(jnp.int32, shape, 0) * shape[1] + lax.broadcasted_iota(
        jnp.int32, shape, 1
    )
    xvals = (2.0 * index.astype(F32) + 1.0) * (1.0 / total) - 1.0
    keep = mask_sq[...].astype(F32)
    here, before = jnp.ones_like(xvals), jnp.zeros_like(xvals)
    gram = jnp.zeros((TERMS, TERMS), F32)
    for k in range(2 * TERMS - 1):
        moment = jnp.sum(here * keep, axis=0, keepdims=True)
        moment = jnp.sum(moment, axis=1, keepdims=True)
        gram = gram + moment * lin[k]
        here, before = next_legendre(k, xvals, here, before), here

    row_id = lax.broadcasted_iota(jnp.int32, (TERMS, 2 * TERMS), 0)
    col_id = lax.broadcasted_iota(jnp.int32, (TERMS, 2 * TERMS), 1)
    eye = jnp.where(row_id + TERMS == col_id, 1.0, 0.0).astype(F32)
    aug = eye + jnp.concatenate([gram, jnp.zeros_like(gram)], axis=1)
    for p in range(TERMS):
        lead = aug[p : p + 1, :] / aug[p : p + 1, p : p + 1]
        aug = jnp.where(row_id == p, lead, aug - aug[:, p : p + 1] * lead)
    inverse = aug[:, TERMS:]

    forward(0)

    step = min(1024, slab_ch)
    base = slab * slab_ch
    for s in range(0, slab_ch, step):
        lane = lax.broadcasted_iota(jnp.int32, (1, step), 1)
        x_s = (2.0 * (base + s + lane).astype(F32) + 1.0) * (1.0 / total) - 1.0
        here, before = jnp.ones_like(x_s), jnp.zeros_like(x_s)
        for n in range(TERMS):
            table[n : n + 1, s : s + step] = here
            here, before = next_legendre(n, x_s, here, before), here
        keep_s = mask_row[:, pl.ds(pl.multiple_of(base + s, LANES), step)].astype(F32)
        hi, mid, lo = split3(table[:, s : s + step] * keep_s)
        w3[0:TERMS, s : s + step] = hi
        w3[TERMS : 2 * TERMS, s : s + step] = mid
        w3[2 * TERMS :, s : s + step] = lo

    forward(1)

    own.wait()
    edge = HALO // LANES

    def snip(start, block):
        r = pl.ds(start, block)
        lane = lax.broadcasted_iota(jnp.int32, (block, LANES), 1)

        def at(ref, t):
            return ref[0:block, (t + edge) * LANES : (t + edge + 1) * LANES]

        def put(ref, t, v):
            ref[0:block, (t + edge) * LANES : (t + edge + 1) * LANES] = v

        def first(t):
            return raw[r, (t + edge) * LANES : (t + edge + 1) * LANES]

        far = WMAX // LANES
        for t in range(-far, tiles + far):
            put(ping, t, jnp.minimum(first(t), 0.5 * (first(t - far) + first(t + far))))
        src, dst = ping, pong
        for k in range(1, PASSES):
            bound = max(LANES, WMAX >> k)
            b = bound // LANES
            d = bound - windows[k]
            back = lax.rem(LANES - d, LANES)
            low_here = lane < LANES - d
            high_here = lane >= d
            reach = 0 if k == PASSES - 1 else b
            left = {}
            right = {}
            for t in range(-reach, tiles + reach):
                for u in (t - b, t - b + 1):
                    if u not in left:
                        left[u] = pltpu.roll(at(src, u), back, 1)
                for u in (t + b - 1, t + b):
                    if u not in right:
                        right[u] = pltpu.roll(at(src, u), d, 1)
                lower = jnp.where(low_here, left[t - b], left[t - b + 1])
                upper = jnp.where(high_here, right[t + b], right[t + b - 1])
                v = jnp.minimum(at(src, t), 0.5 * (lower + upper))
                if k < PASSES - 1:
                    put(dst, t, v)
                else:
                    cols = slice(t * LANES, (t + 1) * LANES)
                    fit[r, cols] = v
            src, dst = dst, src

    def process(c):
        halo_wait(c)
        first_row, part = spans[c]
        block = min(BLOCK, part)
        if part == block:
            snip(first_row, block)
        else:
            def body(i, carry):
                snip(pl.multiple_of(first_row + i * block, 8), block)
                return carry
            lax.fori_loop(0, part // block, body, 0)

    dims = (((1,), (1,)), ((), ()))

    def products(lo, hi):
        whole = fit[lo:hi, :]
        fit_hi = whole.astype(BF16)
        fit_lo = (whole - fit_hi.astype(F32)).astype(BF16)
        rhs3 = lax.dot_general(w3[...], fit_hi, dims, preferred_element_type=F32)
        rhs3 = rhs3 + lax.dot_general(w3[...], fit_lo, dims, preferred_element_type=F32)
        return rhs3[0:TERMS] + (rhs3[TERMS : 2 * TERMS] + rhs3[2 * TERMS :])

    cut = rows * (CHUNKS - 1) // CHUNKS
    for c in range(len(spans)):
        if c + 2 < len(spans):
            forward(c + 2)
        process(c)
        if c in (0, 1) and c + 1 < points:
            relay(c + 1)
        if sum(spans[c]) == cut:
            early = products(0, cut)
    rhs = jnp.concatenate([early, products(cut, rows)], axis=1)
    fold = sums.shape[2] // rows
    high = TERMS // fold
    packed = jnp.concatenate([rhs[i * high : (i + 1) * high] for i in range(fold)], axis=1)
    sums[me] = packed

    def sum_copy(k):
        return pltpu.make_async_remote_copy(
            src_ref=sums.at[me], dst_ref=sums.at[me],
            send_sem=sum_send, recv_sem=sum_recv,
            device_id={"chan": lax.rem(me + k, n_chan)}, device_id_type=MESH,
        )

    for k in range(1, n_chan):
        sum_copy(k).start()

    t_own = table[:, pl.ds(pl.multiple_of(g * ch, LANES), ch)]
    shaped = jnp.zeros_like(t_own)
    for m in range(TERMS):
        shaped = shaped + inverse[:, m : m + 1] * t_own[m : m + 1, :]
    a_hi, a_mid, a_lo = split3(shaped)
    zero = jnp.zeros_like(a_hi)
    right_out[...] = jnp.concatenate(
        [a_hi, a_mid, a_hi, a_lo, a_hi, a_mid, zero, zero], axis=0
    )
    right_copy = pltpu.make_async_copy(right_out, right_hbm, right_sem)
    right_copy.start()

    def sent(ref, sem):
        return pltpu.make_async_remote_copy(
            src_ref=ref, dst_ref=ref, send_sem=sem, recv_sem=own_sem,
            device_id={"chan": me}, device_id_type=MESH,
        )

    if group > 1:
        sent(cube.at[0 : (group - 1) * rows, :], send_sem).wait_send()

    @pl.when(slab < slabs - 1)
    def _():
        sent(raw.at[:, 0:HALO], hop_sem.at[0]).wait_send()

    @pl.when(slab > 0)
    def _():
        sent(raw.at[:, 0:HALO], hop_sem.at[1]).wait_send()

    others = sums.at[0 : n_chan - 1]
    everyone = pltpu.make_async_remote_copy(
        src_ref=others, dst_ref=others, send_sem=sum_send, recv_sem=sum_recv,
        device_id={"chan": me}, device_id_type=MESH,
    )
    everyone.wait_send()
    everyone.wait_recv()
    right_copy.wait()

    for b in range(group):
        tot = sums[b]
        for z in range(1, slabs):
            tot = tot + sums[z * group + b]
        tot = jnp.concatenate(
            [tot[:, i * rows : (i + 1) * rows] for i in range(fold)], axis=0
        )
        hi, mid, lo = (v.astype(F32) for v in split3(tot))
        none = jnp.zeros_like(hi)
        left_side = jnp.concatenate([hi, hi, mid, hi, lo, mid, none, none], axis=0)
        left_out[b * rows : (b + 1) * rows, :] = left_side.T.astype(BF16)


def subtract(cube, left, right, out):
    out[...] = cube[...] - jnp.dot(left[...], right[...], preferred_element_type=F32)


def per_device(cube, windows, mask):
    pix, ch = cube.shape
    n_chan = lax.axis_size("chan")
    total = ch * n_chan
    group = min(n_chan, max(4, HALO // ch))
    slab_ch = group * ch
    rows = pix // group
    wide = slab_ch + 2 * HALO
    fold = max(1, LANES // rows)
    vmem = pl.BlockSpec(memory_space=pltpu.VMEM)
    hbm = pl.BlockSpec(memory_space=pl.ANY)
    dma = pltpu.SemaphoreType.DMA
    chunks = len(chunk_spans(rows))
    lin = jnp.asarray(linearization())
    depth = 8 * TERMS
    left, right = pl.pallas_call(
        functools.partial(kernel, n_chan, group, total),
        out_shape=(
            jax.ShapeDtypeStruct((pix, depth), BF16),
            jax.ShapeDtypeStruct((depth, ch), BF16),
        ),
        in_specs=[hbm, hbm, hbm, hbm, hbm],
        out_specs=(vmem, hbm),
        scratch_shapes=[
            pltpu.SMEM(windows.shape, jnp.int32),
            pltpu.VMEM((depth, ch), BF16),
            pltpu.VMEM((total // LANES, LANES), jnp.int32),
            pltpu.VMEM((1, total), jnp.int32),
            pltpu.VMEM(lin.shape, F32),
            pltpu.VMEM((rows, wide), F32),
            pltpu.VMEM((BLOCK, wide), F32),
            pltpu.VMEM((BLOCK, wide), F32),
            pltpu.VMEM((rows, slab_ch), F32),
            pltpu.VMEM((TERMS, slab_ch), F32),
            pltpu.VMEM((3 * TERMS, slab_ch), BF16),
            pltpu.VMEM((n_chan, TERMS // fold, rows * fold), F32),
            dma((4,)), dma, pltpu.SemaphoreType.REGULAR((2,)), dma, dma, dma((2,)),
            dma((chunks, group)), dma((chunks,)), dma((chunks,)),
            dma, dma,
        ],
        compiler_params=pltpu.CompilerParams(
            collective_id=0, has_side_effects=True
        ),
    )(windows, cube, mask.reshape(-1, LANES), mask.reshape(1, total), lin)
    step = max(pix // SPLIT, 16)
    return pl.pallas_call(
        subtract,
        grid=(pix // step,),
        out_shape=jax.ShapeDtypeStruct((pix, ch), F32),
        in_specs=[
            pl.BlockSpec((step, ch), lambda i: (i, 0)),
            pl.BlockSpec((step, depth), lambda i: (i, 0)),
            pl.BlockSpec((depth, ch), lambda i: (0, 0)),
        ],
        out_specs=pl.BlockSpec((step, ch), lambda i: (i, 0)),
    )(cube, left, right)


def solution(mesh):
    placed = (P("pix", "chan"), P(), P())
    return jax.shard_map(
        per_device, mesh=mesh, in_specs=placed, out_specs=P("pix", "chan"), check_vma=False
    )
```

profile of v0, /device:TPU:0, one launch (start us, length us, event | category | flops | bytes accessed | tf_op | source)
XLA Modules:
  0.0 31.1 jit_solution(13932147351211788028)
XLA Ops:
  0.0 28.7 %shard_map.46 = (bf16[256,128]{1,0:T(8,128)(2,1)}, bf16[128,1024]{1,0:T(8,128)(2,1)}) custom-call(s32[8]{0:T(128)} %windows_hbm.1, f32[256,1024]{1,0:T(8,128)} %cube.3, s32[128,128]{1,0:T(8,128)} %bitcast.2, s32[1,16384]{1,0:T(1,128)} %bitcast.3, f32[31,16,16]{2,1,0:T(8,128)} %constant.2.clone.lin_hbm), custom_call_target="tpu_custom_call" | custom-call | tf_op jit(solution)/shard_map/pallas_call | solution.py:447
  28.7 2.4 %shard_map.47 = f32[256,1024]{1,0:T(8,128)} custom-call(f32[256,1024]{1,0:T(8,128)} %cube.3, bf16[256,128]{1,0:T(8,128)(2,1)} %get-tuple-element.7.left, bf16[128,1024]{1,0:T(8,128)(2,1)} %get-tuple-element.8.right), custom_call_target="tpu_custom_call" | custom-call | tf_op jit(solution)/shard_map/pallas_call | solution.py:477
where the time goes:
time: 31.3 us; the launch traced here: 31.1 us
  Pallas kernels  31.1 us (99%)
    pallas_call x1, Pallas kernels, per_device(): pl.pallas_call(functools.partial(kernel, n_chan, group, total), out_shape...  28.7 us
    pallas_call x1, Pallas kernels, per_device(): pl.pallas_call(subtract, grid=(pix // step,), out_shape=jax.ShapeDtypeStr...  2.39 us

commit v1 on v0

--- a/solution.py
+++ b/solution.py
@@ -14,22 +14,17 @@
 WMAX = 1024
 HALO = 2 * WMAX
 LANES = 128
-BLOCK = 16
-CHUNKS = 4
-SPLIT = 2
-TAIL = True
+CHUNKS = 8
+LAG = 4
+SPLIT = 4
 MESH = pl.DeviceIdType.MESH
 F32 = jnp.float32
 BF16 = jnp.bfloat16
 
 
 def chunk_spans(rows):
-    part = rows // CHUNKS
-    sizes = [part] * CHUNKS
-    if TAIL and part >= 16:
-        sizes[-1:] = [part // 2, part // 2]
-    starts = [sum(sizes[:i]) for i in range(len(sizes))]
-    return list(zip(starts, sizes))
+    part = max(8, rows // CHUNKS)
+    return [(start, part) for start in range(0, rows, part)]
 
 
 def linearization():
@@ -63,9 +58,9 @@
 def kernel(
     n_chan, group, total,
     windows_hbm, cube, mask_sq_hbm, mask_row_hbm, lin_hbm,
-    left_out, right_hbm,
-    windows, right_out, mask_sq, mask_row, lin, raw, ping, pong, fit, table, w3, sums,
-    load_sem, right_sem, token, own_sem, send_sem, hop_sem, recv_sem, up_sem, down_sem, sum_send, sum_recv,
+    left_out, right_out, mine,
+    windows, mask_sq, mask_row, lin, raw, ping, pong, fit, table, w3, sums,
+    load_sem, mine_sem, token, own_sem, send_sem, hop_sem, recv_sem, up_sem, down_sem, sum_send, sum_recv,
 ):
     pix, ch = cube.shape
     rows = raw.shape[0]
@@ -109,6 +104,7 @@
     own = pltpu.make_async_copy(
         cube.at[pl.ds(own_rows, rows), :], raw.at[:, pl.ds(own_col, ch)], own_sem
     )
+    kept = pltpu.make_async_copy(cube, mine, mine_sem)
     for copy in loads:
         copy.start()
     own.start()
@@ -197,19 +193,22 @@
                 def _():
                     hop(c, b, False, True).start()
 
-    def forward(c):
+    def pass_on(c, b):
+        slab_recv(c, b).wait_recv()
+        if goes_up(b):
+            @pl.when(slab < slabs - 1)
+            def _():
+                hop(c, b, True, False).start()
+        if goes_down(b):
+            @pl.when(slab > 0)
+            def _():
+                hop(c, b, False, False).start()
+
+    def forward(c, near):
         for b in range(group):
-            @pl.when(g != b)
+            @pl.when((g != b) & ((g // 2 == b // 2) == near))
             def _():
-                slab_recv(c, b).wait_recv()
-                if goes_up(b):
-                    @pl.when(slab < slabs - 1)
-                    def _():
-                        hop(c, b, True, False).start()
-                if goes_down(b):
-                    @pl.when(slab > 0)
-                    def _():
-                        hop(c, b, False, False).start()
+                pass_on(c, b)
 
     def halo_wait(c):
         def arrived(col, sem):
@@ -234,6 +233,7 @@
             def _():
                 slab_send(c, b).start()
         own_hops(c)
+    kept.start()
     relay(0)
     for copy in loads:
         copy.wait()
@@ -260,8 +260,6 @@
         lead = aug[p : p + 1, :] / aug[p : p + 1, p : p + 1]
         aug = jnp.where(row_id == p, lead, aug - aug[:, p : p + 1] * lead)
     inverse = aug[:, TERMS:]
-
-    forward(0)
 
     step = min(1024, slab_ch)
     base = slab * slab_ch
@@ -278,7 +276,8 @@
         w3[TERMS : 2 * TERMS, s : s + step] = mid
         w3[2 * TERMS :, s : s + step] = lo
 
-    forward(1)
+    for c in range(len(spans)):
+        forward(c, True)
 
     own.wait()
     edge = HALO // LANES
@@ -329,15 +328,7 @@
 
     def process(c):
         halo_wait(c)
-        first_row, part = spans[c]
-        block = min(BLOCK, part)
-        if part == block:
-            snip(first_row, block)
-        else:
-            def body(i, carry):
-                snip(pl.multiple_of(first_row + i * block, 8), block)
-                return carry
-            lax.fori_loop(0, part // block, body, 0)
+        snip(*spans[c])
 
     dims = (((1,), (1,)), ((), ()))
 
@@ -349,15 +340,18 @@
         rhs3 = rhs3 + lax.dot_general(w3[...], fit_lo, dims, preferred_element_type=F32)
         return rhs3[0:TERMS] + (rhs3[TERMS : 2 * TERMS] + rhs3[2 * TERMS :])
 
-    cut = rows * (CHUNKS - 1) // CHUNKS
-    for c in range(len(spans)):
-        if c + 2 < len(spans):
-            forward(c + 2)
-        process(c)
-        if c in (0, 1) and c + 1 < points:
-            relay(c + 1)
-        if sum(spans[c]) == cut:
-            early = products(0, cut)
+    count = len(spans)
+    lag = min(LAG, count)
+    cut = spans[-1][0] - spans[-1][1]
+    for c in range(count + lag):
+        if c < count:
+            forward(c, False)
+        if c >= lag:
+            process(c - lag)
+            if c - lag < points - 1:
+                relay(c - lag + 1)
+            if c - lag == count - 3:
+                early = products(0, cut)
     rhs = jnp.concatenate([early, products(cut, rows)], axis=1)
     fold = sums.shape[2] // rows
     high = TERMS // fold
@@ -383,8 +377,6 @@
     right_out[...] = jnp.concatenate(
         [a_hi, a_mid, a_hi, a_lo, a_hi, a_mid, zero, zero], axis=0
     )
-    right_copy = pltpu.make_async_copy(right_out, right_hbm, right_sem)
-    right_copy.start()
 
     def sent(ref, sem):
         return pltpu.make_async_remote_copy(
@@ -410,7 +402,7 @@
     )
     everyone.wait_send()
     everyone.wait_recv()
-    right_copy.wait()
+    kept.wait()
 
     for b in range(group):
         tot = sums[b]
@@ -425,8 +417,13 @@
         left_out[b * rows : (b + 1) * rows, :] = left_side.T.astype(BF16)
 
 
-def subtract(cube, left, right, out):
-    out[...] = cube[...] - jnp.dot(left[...], right[...], preferred_element_type=F32)
+def subtract(cube, left, right, out, buf, sem):
+    step = max(cube.shape[0] // SPLIT, 16)
+    for start in range(0, cube.shape[0], step):
+        r = pl.ds(start, step)
+        buf[r, :] = cube[r, :] - jnp.dot(left[r, :], right[...], preferred_element_type=F32)
+        pltpu.make_async_copy(buf.at[r, :], out.at[r, :], sem).start()
+    pltpu.make_async_copy(buf, out, sem).wait()
 
 
 def per_device(cube, windows, mask):
@@ -442,25 +439,26 @@
     hbm = pl.BlockSpec(memory_space=pl.ANY)
     dma = pltpu.SemaphoreType.DMA
     chunks = len(chunk_spans(rows))
+    part = rows // chunks
     lin = jnp.asarray(linearization())
     depth = 8 * TERMS
-    left, right = pl.pallas_call(
+    kept = pl.pallas_call(
         functools.partial(kernel, n_chan, group, total),
         out_shape=(
-            jax.ShapeDtypeStruct((pix, depth), BF16),
-            jax.ShapeDtypeStruct((depth, ch), BF16),
+            pltpu.VMEM((pix, depth), BF16),
+            pltpu.VMEM((depth, ch), BF16),
+            pltpu.VMEM((pix, ch), F32),
         ),
         in_specs=[hbm, hbm, hbm, hbm, hbm],
-        out_specs=(vmem, hbm),
+        out_specs=(vmem, vmem, vmem),
         scratch_shapes=[
             pltpu.SMEM(windows.shape, jnp.int32),
-            pltpu.VMEM((depth, ch), BF16),
             pltpu.VMEM((total // LANES, LANES), jnp.int32),
             pltpu.VMEM((1, total), jnp.int32),
             pltpu.VMEM(lin.shape, F32),
             pltpu.VMEM((rows, wide), F32),
-            pltpu.VMEM((BLOCK, wide), F32),
-            pltpu.VMEM((BLOCK, wide), F32),
+            pltpu.VMEM((part, wide), F32),
+            pltpu.VMEM((part, wide), F32),
             pltpu.VMEM((rows, slab_ch), F32),
             pltpu.VMEM((TERMS, slab_ch), F32),
             pltpu.VMEM((3 * TERMS, slab_ch), BF16),
@@ -473,18 +471,14 @@
             collective_id=0, has_side_effects=True
         ),
     )(windows, cube, mask.reshape(-1, LANES), mask.reshape(1, total), lin)
-    step = max(pix // SPLIT, 16)
+    left, right, mine = (pltpu.with_memory_space_constraint(a, pltpu.VMEM) for a in kept)
     return pl.pallas_call(
         subtract,
-        grid=(pix // step,),
         out_shape=jax.ShapeDtypeStruct((pix, ch), F32),
-        in_specs=[
-            pl.BlockSpec((step, ch), lambda i: (i, 0)),
-            pl.BlockSpec((step, depth), lambda i: (i, 0)),
-            pl.BlockSpec((depth, ch), lambda i: (0, 0)),
-        ],
-        out_specs=pl.BlockSpec((step, ch), lambda i: (i, 0)),
-    )(cube, left, right)
+        in_specs=[vmem, vmem, vmem],
+        out_specs=hbm,
+        scratch_shapes=[pltpu.VMEM((pix, ch), F32), dma],
+    )(mine, left, right)
 
 
 def solution(mesh):

time: 31.3 us -> 29.2 us (0.933)
  Pallas kernels: 31.1 us -> 29 us
    pallas_call x1, Pallas kernels: 2.39 us -> 1.16 us  [per_device(): pl.pallas_call(subtract, out_shape=jax.ShapeDtypeStruct((pix, ch), F32),...]
    pallas_call x1, Pallas kernels: 28.7 us -> 27.9 us  [per_device(): pl.pallas_call(functools.partial(kernel, n_chan, group, total), out_shape...]
where the time goes in v1:
time: 29.2 us; the launch traced here: 29 us
  Pallas kernels  29 us (99%)
    pallas_call x1, Pallas kernels, per_device(): pl.pallas_call(functools.partial(kernel, n_chan, group, total), out_shape...  27.9 us
    pallas_call x1, Pallas kernels, per_device(): pl.pallas_call(subtract, out_shape=jax.ShapeDtypeStruct((pix, ch), F32),...  1.16 us

profile of v1, /device:TPU:0, one launch (start us, length us, event | category | flops | bytes accessed | tf_op | source)
XLA Modules:
  0.0 29.0 jit_solution(16386096880902445990)
XLA Ops:
  0.0 27.9 %shard_map.46 = (bf16[256,128]{1,0:T(8,128)(2,1)S(1)}, bf16[128,1024]{1,0:T(8,128)(2,1)S(1)}, f32[256,1024]{1,0:T(8,128)S(1)}) custom-call(s32[8]{0:T(128)} %windows_hbm.1, f32[256,1024]{1,0:T(8,128)} %cube.1, s32[128,128]{1,0:T(8,128)} %bitcast.2, s32[1,16384]{1,0:T(1,128)} %bitcast.3, f32[31,16,16]{2,1,0:T(8,128)} %constant.2.clone.lin_hbm), custom_call_target="tpu_custom_call" | custom-call | tf_op jit(solution)/shard_map/pallas_call | solution.py:445
  27.9 1.2 %shard_map.47 = f32[256,1024]{1,0:T(8,128)} custom-call(f32[256,1024]{1,0:T(8,128)S(1)} %get-tuple-element.8.cube, bf16[256,128]{1,0:T(8,128)(2,1)S(1)} %get-tuple-element.9.left, bf16[128,1024]{1,0:T(8,128)(2,1)S(1)} %get-tuple-element.10.right), custom_call_target="tpu_custom_call" | custom-call | tf_op jit(solution)/shard_map/pallas_call | solution.py:475

commit v2 on v1

--- a/solution.py
+++ b/solution.py
@@ -15,7 +15,8 @@
 HALO = 2 * WMAX
 LANES = 128
 CHUNKS = 8
-LAG = 4
+LAG = 3
+AHEAD = 3
 SPLIT = 4
 MESH = pl.DeviceIdType.MESH
 F32 = jnp.float32
@@ -60,7 +61,7 @@
     windows_hbm, cube, mask_sq_hbm, mask_row_hbm, lin_hbm,
     left_out, right_out, mine,
     windows, mask_sq, mask_row, lin, raw, ping, pong, fit, table, w3, sums,
-    load_sem, mine_sem, token, own_sem, send_sem, hop_sem, recv_sem, up_sem, down_sem, sum_send, sum_recv,
+    load_sem, own_sem, token, send_sem, near_sem, far_sem, halo_sem, sum_send, sum_recv,
 ):
     pix, ch = cube.shape
     rows = raw.shape[0]
@@ -104,7 +105,7 @@
     own = pltpu.make_async_copy(
         cube.at[pl.ds(own_rows, rows), :], raw.at[:, pl.ds(own_col, ch)], own_sem
     )
-    kept = pltpu.make_async_copy(cube, mine, mine_sem)
+    kept = pltpu.make_async_copy(cube, mine, own_sem)
     for copy in loads:
         copy.start()
     own.start()
@@ -120,7 +121,7 @@
     near = group - 1 + jnp.where(slab > 0, 1, 0) + jnp.where(slab < slabs - 1, 1, 0)
     pl.semaphore_wait(barrier, near)
 
-    points = min(slabs, 3)
+    points = min(slabs, len(spans))
 
     def relay(point):
         for up in (True, False):
@@ -143,38 +144,44 @@
     def chunk(c):
         return pl.ds(*spans[c])
 
-    def slab_send(c, b):
+    def remote(src, dst, recv_sem, to):
         return pltpu.make_async_remote_copy(
-            src_ref=cube.at[pl.ds(b * rows + spans[c][0], spans[c][1]), :],
-            dst_ref=raw.at[chunk(c), pl.ds(own_col, ch)],
-            send_sem=send_sem, recv_sem=recv_sem.at[c, g],
-            device_id=peer(b), device_id_type=MESH,
-        )
-
-    def slab_recv(c, b):
-        return pltpu.make_async_remote_copy(
-            src_ref=cube.at[chunk(c), :],
-            dst_ref=raw.at[chunk(c), pl.ds(HALO + b * ch, ch)],
-            send_sem=send_sem, recv_sem=recv_sem.at[c, b],
-            device_id=peer(b), device_id_type=MESH,
+            src_ref=src, dst_ref=dst, send_sem=send_sem, recv_sem=recv_sem,
+            device_id=to, device_id_type=MESH,
+        )
+
+    def near_send(b):
+        return remote(
+            cube.at[b * rows : (b + 1) * rows, :], raw.at[:, pl.ds(own_col, ch)], near_sem, peer(b)
+        )
+
+    def far_send(c, b):
+        return remote(
+            cube.at[pl.ds(b * rows + spans[c][0], spans[c][1]), :],
+            raw.at[chunk(c), pl.ds(own_col, ch)], far_sem.at[c], peer(b),
         )
 
     def hop(c, b, up, from_own):
-        if up:
-            col = b * ch - (slab_ch - HALO)
-            sem, to = up_sem.at[c], me + group
-        else:
-            col = HALO + slab_ch + b * ch
-            sem, to = down_sem.at[c], me - group
+        col = b * ch - (slab_ch - HALO) if up else HALO + slab_ch + b * ch
         if from_own:
             src = cube.at[pl.ds(pl.multiple_of(own_rows + spans[c][0], 8), spans[c][1]), :]
         else:
             src = raw.at[chunk(c), pl.ds(HALO + b * ch, ch)]
-        return pltpu.make_async_remote_copy(
-            src_ref=src, dst_ref=raw.at[chunk(c), pl.ds(col, ch)],
-            send_sem=hop_sem.at[0 if up else 1], recv_sem=sem,
-            device_id={"chan": to}, device_id_type=MESH,
-        )
+        to = {"chan": me + group if up else me - group}
+        return remote(src, raw.at[chunk(c), pl.ds(col, ch)], halo_sem.at[c], to)
+
+    def amount(r, width, recv_sem):
+        ref = raw.at[r, 0:width]
+        return remote(ref, ref, recv_sem, {"chan": me})
+
+    inner = (slab > 0) & (slab < slabs - 1)
+
+    def sided(wait):
+        if slabs > 1:
+            pl.when(inner)(lambda: wait(2 * HALO))
+            pl.when(jnp.logical_not(inner))(lambda: wait(HALO))
+        else:
+            wait(0)
 
     def goes_up(b):
         return b * ch >= slab_ch - HALO
@@ -194,7 +201,6 @@
                     hop(c, b, False, True).start()
 
     def pass_on(c, b):
-        slab_recv(c, b).wait_recv()
         if goes_up(b):
             @pl.when(slab < slabs - 1)
             def _():
@@ -204,36 +210,39 @@
             def _():
                 hop(c, b, False, False).start()
 
-    def forward(c, near):
+    def forward_near():
+        amount(pl.ds(0, rows), ch, near_sem).wait_recv()
+        for c in range(len(spans)):
+            if c >= AHEAD:
+                own_hops(c)
+            for b in range(group):
+                @pl.when((g != b) & (g // 2 == b // 2))
+                def _():
+                    pass_on(c, b)
+
+    def forward_far(c):
+        amount(chunk(c), (group - 2) * ch, far_sem.at[c]).wait_recv()
         for b in range(group):
-            @pl.when((g != b) & ((g // 2 == b // 2) == near))
+            @pl.when(g // 2 != b // 2)
             def _():
                 pass_on(c, b)
 
     def halo_wait(c):
-        def arrived(col, sem):
-            return pltpu.make_async_remote_copy(
-                src_ref=raw.at[chunk(c), pl.ds(col, HALO)],
-                dst_ref=raw.at[chunk(c), pl.ds(col, HALO)],
-                send_sem=hop_sem.at[0], recv_sem=sem,
-                device_id={"chan": me}, device_id_type=MESH,
-            )
-
-        @pl.when(slab > 0)
-        def _():
-            arrived(0, up_sem.at[c]).wait_recv()
-
-        @pl.when(slab < slabs - 1)
-        def _():
-            arrived(HALO + slab_ch, down_sem.at[c]).wait_recv()
+        if slabs > 1:
+            sided(lambda width: amount(chunk(c), width, halo_sem.at[c]).wait_recv())
 
     for c in range(len(spans)):
         for b in range(group):
-            @pl.when(g != b)
+            @pl.when(g // 2 != b // 2)
             def _():
-                slab_send(c, b).start()
-        own_hops(c)
-    kept.start()
+                far_send(c, b).start()
+        if c == 0:
+            for b in range(group):
+                @pl.when((g != b) & (g // 2 == b // 2))
+                def _():
+                    near_send(b).start()
+        if c < AHEAD:
+            own_hops(c)
     relay(0)
     for copy in loads:
         copy.wait()
@@ -261,25 +270,39 @@
         aug = jnp.where(row_id == p, lead, aug - aug[:, p : p + 1] * lead)
     inverse = aug[:, TERMS:]
 
-    step = min(1024, slab_ch)
+    half = slab_ch // 2
+    step = min(1024, half)
     base = slab * slab_ch
-    for s in range(0, slab_ch, step):
-        lane = lax.broadcasted_iota(jnp.int32, (1, step), 1)
-        x_s = (2.0 * (base + s + lane).astype(F32) + 1.0) * (1.0 / total) - 1.0
-        here, before = jnp.ones_like(x_s), jnp.zeros_like(x_s)
-        for n in range(TERMS):
-            table[n : n + 1, s : s + step] = here
-            here, before = next_legendre(n, x_s, here, before), here
-        keep_s = mask_row[:, pl.ds(pl.multiple_of(base + s, LANES), step)].astype(F32)
-        hi, mid, lo = split3(table[:, s : s + step] * keep_s)
-        w3[0:TERMS, s : s + step] = hi
-        w3[TERMS : 2 * TERMS, s : s + step] = mid
-        w3[2 * TERMS :, s : s + step] = lo
-
-    for c in range(len(spans)):
-        forward(c, True)
-
-    own.wait()
+
+    def weigh(q):
+        parts = []
+        for s in (q * step, half + q * step):
+            lane = lax.broadcasted_iota(jnp.int32, (1, step), 1)
+            x_s = (2.0 * (base + s + lane).astype(F32) + 1.0) * (1.0 / total) - 1.0
+            here, before = jnp.ones_like(x_s), jnp.zeros_like(x_s)
+            for n in range(TERMS):
+                table[n : n + 1, s : s + step] = here
+                here, before = next_legendre(n, x_s, here, before), here
+            keep_s = mask_row[:, pl.ds(pl.multiple_of(base + s, LANES), step)].astype(F32)
+            parts += [v.astype(F32) for v in split3(table[:, s : s + step] * keep_s)]
+        parts.append(jnp.zeros((2 * TERMS, step), F32))
+        w3[q * step : (q + 1) * step, :] = jnp.concatenate(parts, axis=0).T.astype(BF16)
+
+    def shape_own():
+        t_own = table[:, pl.ds(pl.multiple_of(g * ch, LANES), ch)]
+        shaped = jnp.zeros_like(t_own)
+        for m in range(TERMS):
+            shaped = shaped + inverse[:, m : m + 1] * t_own[m : m + 1, :]
+        a_hi, a_mid, a_lo = split3(shaped)
+        zero = jnp.zeros_like(a_hi)
+        right_out[...] = jnp.concatenate(
+            [a_hi, a_mid, a_hi, a_lo, a_hi, a_mid, zero, zero], axis=0
+        )
+
+    forward_near()
+    kept.start()
+    if points > 1:
+        relay(1)
     edge = HALO // LANES
 
     def snip(start, block):
@@ -330,91 +353,100 @@
         halo_wait(c)
         snip(*spans[c])
 
-    dims = (((1,), (1,)), ((), ()))
-
-    def products(lo, hi):
-        whole = fit[lo:hi, :]
-        fit_hi = whole.astype(BF16)
-        fit_lo = (whole - fit_hi.astype(F32)).astype(BF16)
-        rhs3 = lax.dot_general(w3[...], fit_hi, dims, preferred_element_type=F32)
-        rhs3 = rhs3 + lax.dot_general(w3[...], fit_lo, dims, preferred_element_type=F32)
-        return rhs3[0:TERMS] + (rhs3[TERMS : 2 * TERMS] + rhs3[2 * TERMS :])
+    part = spans[0][1]
+    lanes = lax.broadcasted_iota(jnp.int32, (part, LANES), 1)
+    place = lanes // TERMS
+
+    def gather(v):
+        for shift in (4 * TERMS, 2 * TERMS, TERMS):
+            v = v + pltpu.roll(v, shift, 1)
+        return v
+
+    def products(c):
+        whole = fit[chunk(c), :]
+        hi = whole.astype(BF16).astype(F32)
+        lo = whole - hi
+        both = jnp.concatenate(
+            [hi[:, 0:half], lo[:, 0:half], hi[:, half:], lo[:, half:]], axis=0
+        ).astype(BF16)
+        rhs = jnp.dot(both, w3[...], preferred_element_type=F32)
+        low = rhs[0:part] + rhs[part : 2 * part]
+        high = rhs[2 * part : 3 * part] + rhs[3 * part :]
+        return jnp.where(lanes < 3 * TERMS, low, high)
+
+    def send_sums(late):
+        mine_at = sums.at[late * n_chan + me]
+        for k in range(1, n_chan):
+            pltpu.make_async_remote_copy(
+                src_ref=mine_at, dst_ref=mine_at,
+                send_sem=sum_send, recv_sem=sum_recv.at[late],
+                device_id={"chan": lax.rem(me + k, n_chan)}, device_id_type=MESH,
+            ).start()
 
     count = len(spans)
     lag = min(LAG, count)
-    cut = spans[-1][0] - spans[-1][1]
+    pairs = half // step
+    early = jnp.zeros((part, LANES), F32)
+    filled = raw.at[:, 0 : (group + 1) * ch]
     for c in range(count + lag):
         if c < count:
-            forward(c, False)
+            forward_far(c)
+        if c < lag:
+            for q in range(c * pairs // lag, (c + 1) * pairs // lag):
+                weigh(q)
+            if c == lag - 1:
+                shape_own()
+        if 2 <= c + 1 < points:
+            relay(c + 1)
+        if c == lag:
+            pltpu.make_async_copy(filled, filled, own_sem).wait()
         if c >= lag:
-            process(c - lag)
-            if c - lag < points - 1:
-                relay(c - lag + 1)
-            if c - lag == count - 3:
-                early = products(0, cut)
-    rhs = jnp.concatenate([early, products(cut, rows)], axis=1)
-    fold = sums.shape[2] // rows
-    high = TERMS // fold
-    packed = jnp.concatenate([rhs[i * high : (i + 1) * high] for i in range(fold)], axis=1)
-    sums[me] = packed
-
-    def sum_copy(k):
+            done = c - lag
+            process(done)
+            found = products(done)
+            if done < count - 1:
+                early = jnp.where(place == done, gather(found), early)
+            if done == count - 2:
+                sums[me] = early
+                send_sums(0)
+    sums[n_chan + me] = found
+    send_sums(1)
+
+    sided(lambda width: amount(pl.ds(0, rows), (group - 1) * ch + width, near_sem).wait_send())
+
+    def sums_wait(first, blocks, recv):
+        ref = sums.at[first : first + blocks]
         return pltpu.make_async_remote_copy(
-            src_ref=sums.at[me], dst_ref=sums.at[me],
-            send_sem=sum_send, recv_sem=sum_recv,
-            device_id={"chan": lax.rem(me + k, n_chan)}, device_id_type=MESH,
-        )
-
-    for k in range(1, n_chan):
-        sum_copy(k).start()
-
-    t_own = table[:, pl.ds(pl.multiple_of(g * ch, LANES), ch)]
-    shaped = jnp.zeros_like(t_own)
-    for m in range(TERMS):
-        shaped = shaped + inverse[:, m : m + 1] * t_own[m : m + 1, :]
-    a_hi, a_mid, a_lo = split3(shaped)
-    zero = jnp.zeros_like(a_hi)
-    right_out[...] = jnp.concatenate(
-        [a_hi, a_mid, a_hi, a_lo, a_hi, a_mid, zero, zero], axis=0
-    )
-
-    def sent(ref, sem):
-        return pltpu.make_async_remote_copy(
-            src_ref=ref, dst_ref=ref, send_sem=sem, recv_sem=own_sem,
+            src_ref=ref, dst_ref=ref, send_sem=sum_send, recv_sem=recv,
             device_id={"chan": me}, device_id_type=MESH,
         )
 
-    if group > 1:
-        sent(cube.at[0 : (group - 1) * rows, :], send_sem).wait_send()
-
-    @pl.when(slab < slabs - 1)
-    def _():
-        sent(raw.at[:, 0:HALO], hop_sem.at[0]).wait_send()
-
-    @pl.when(slab > 0)
-    def _():
-        sent(raw.at[:, 0:HALO], hop_sem.at[1]).wait_send()
-
-    others = sums.at[0 : n_chan - 1]
-    everyone = pltpu.make_async_remote_copy(
-        src_ref=others, dst_ref=others, send_sem=sum_send, recv_sem=sum_recv,
-        device_id={"chan": me}, device_id_type=MESH,
-    )
-    everyone.wait_send()
-    everyone.wait_recv()
-    kept.wait()
-
+    def put_left(start, spread):
+        spread = gather(spread)
+        hi, mid, lo = (v.astype(F32) for v in split3(spread))
+        spot = lax.broadcasted_iota(jnp.int32, spread.shape, 1) // TERMS
+        picked = jnp.where(spot == 4, lo, jnp.zeros_like(lo))
+        picked = jnp.where((spot == 2) | (spot == 5), mid, picked)
+        picked = jnp.where((spot < 2) | (spot == 3), hi, picked)
+        left_out[start : start + spread.shape[0], :] = picked.astype(BF16)
+
+    def over_slabs(late, b):
+        tot = sums[late * n_chan + b]
+        for z in range(1, slabs):
+            tot = tot + sums[late * n_chan + z * group + b]
+        return tot
+
+    sums_wait(0, n_chan - 1, sum_recv.at[0]).wait_recv()
     for b in range(group):
-        tot = sums[b]
-        for z in range(1, slabs):
-            tot = tot + sums[z * group + b]
-        tot = jnp.concatenate(
-            [tot[:, i * rows : (i + 1) * rows] for i in range(fold)], axis=0
-        )
-        hi, mid, lo = (v.astype(F32) for v in split3(tot))
-        none = jnp.zeros_like(hi)
-        left_side = jnp.concatenate([hi, hi, mid, hi, lo, mid, none, none], axis=0)
-        left_out[b * rows : (b + 1) * rows, :] = left_side.T.astype(BF16)
+        tot = over_slabs(0, b)
+        put_left(
+            b * rows,
+            jnp.concatenate([jnp.where(place == c, tot, 0.0) for c in range(count - 1)], axis=0),
+        )
+    sums_wait(0, 2 * (n_chan - 1), sum_recv.at[0]).wait_send()
+    sums_wait(0, n_chan - 1, sum_recv.at[1]).wait_recv()
+    for b in range(group):
+        put_left(b * rows + spans[-1][0], over_slabs(1, b))
 
 
 def subtract(cube, left, right, out, buf, sem):
@@ -434,7 +466,6 @@
     slab_ch = group * ch
     rows = pix // group
     wide = slab_ch + 2 * HALO
-    fold = max(1, LANES // rows)
     vmem = pl.BlockSpec(memory_space=pltpu.VMEM)
     hbm = pl.BlockSpec(memory_space=pl.ANY)
     dma = pltpu.SemaphoreType.DMA
@@ -461,11 +492,10 @@
             pltpu.VMEM((part, wide), F32),
             pltpu.VMEM((rows, slab_ch), F32),
             pltpu.VMEM((TERMS, slab_ch), F32),
-            pltpu.VMEM((3 * TERMS, slab_ch), BF16),
-            pltpu.VMEM((n_chan, TERMS // fold, rows * fold), F32),
-            dma((4,)), dma, pltpu.SemaphoreType.REGULAR((2,)), dma, dma, dma((2,)),
-            dma((chunks, group)), dma((chunks,)), dma((chunks,)),
-            dma, dma,
+            pltpu.VMEM((slab_ch // 2, LANES), BF16),
+            pltpu.VMEM((2 * n_chan, part, LANES), F32),
+            dma((4,)), dma, pltpu.SemaphoreType.REGULAR((2,)), dma, dma,
+            dma((chunks,)), dma((chunks,)), dma, dma((2,)),
         ],
         compiler_params=pltpu.CompilerParams(
             collective_id=0, has_side_effects=True

time: 29.2 us -> 28.6 us (0.979)
  Pallas kernels: 29 us -> 28.5 us
    pallas_call x1, Pallas kernels: 27.9 us -> 27.3 us  [per_device(): pl.pallas_call(functools.partial(kernel, n_chan, group, total), out_shape...]
where the time goes in v2:
time: 28.6 us; the launch traced here: 28.5 us
  Pallas kernels  28.5 us (100%)
    pallas_call x1, Pallas kernels, per_device(): pl.pallas_call(functools.partial(kernel, n_chan, group, total), out_shape...  27.3 us
    pallas_call x1, Pallas kernels, per_device(): pl.pallas_call(subtract, out_shape=jax.ShapeDtypeStruct((pix, ch), F32),...  1.16 us

profile of v2, /device:TPU:0, one launch (start us, length us, event | category | flops | bytes accessed | tf_op | source)
XLA Modules:
  0.0 28.5 jit_solution(998770604162971099)
XLA Ops:
  0.0 27.3 %shard_map.46 = (bf16[256,128]{1,0:T(8,128)(2,1)S(1)}, bf16[128,1024]{1,0:T(8,128)(2,1)S(1)}, f32[256,1024]{1,0:T(8,128)S(1)}) custom-call(s32[8]{0:T(128)} %windows_hbm.1, f32[256,1024]{1,0:T(8,128)} %cube.1, s32[128,128]{1,0:T(8,128)} %bitcast.2, s32[1,16384]{1,0:T(1,128)} %bitcast.3, f32[31,16,16]{2,1,0:T(8,128)} %constant.2.clone.lin_hbm), custom_call_target="tpu_custom_call" | custom-call | tf_op jit(solution)/shard_map/pallas_call | solution.py:476
  27.3 1.2 %shard_map.47 = f32[256,1024]{1,0:T(8,128)} custom-call(f32[256,1024]{1,0:T(8,128)S(1)} %get-tuple-element.8.cube, bf16[256,128]{1,0:T(8,128)(2,1)S(1)} %get-tuple-element.9.left, bf16[128,1024]{1,0:T(8,128)(2,1)S(1)} %get-tuple-element.10.right), custom_call_target="tpu_custom_call" | custom-call | tf_op jit(solution)/shard_map/pallas_call | solution.py:505

commit v3 on v2

--- a/solution.py
+++ b/solution.py
@@ -17,7 +17,8 @@
 CHUNKS = 8
 LAG = 3
 AHEAD = 3
-SPLIT = 4
+PIECES = 2
+WINDOW = 10
 MESH = pl.DeviceIdType.MESH
 F32 = jnp.float32
 BF16 = jnp.bfloat16
@@ -69,6 +70,8 @@
     tiles = slab_ch // LANES
     slabs = n_chan // group
     spans = chunk_spans(rows)
+    pieces = far_sem.shape[1]
+    bit = ch // pieces
     me = lax.axis_index("chan")
     slab = me // group
     g = lax.rem(me, group)
@@ -155,20 +158,22 @@
             cube.at[b * rows : (b + 1) * rows, :], raw.at[:, pl.ds(own_col, ch)], near_sem, peer(b)
         )
 
-    def far_send(c, b):
+    def far_send(c, p, b):
         return remote(
-            cube.at[pl.ds(b * rows + spans[c][0], spans[c][1]), :],
-            raw.at[chunk(c), pl.ds(own_col, ch)], far_sem.at[c], peer(b),
-        )
-
-    def hop(c, b, up, from_own):
-        col = b * ch - (slab_ch - HALO) if up else HALO + slab_ch + b * ch
+            cube.at[pl.ds(b * rows + spans[c][0], spans[c][1]), pl.ds(p * bit, bit)],
+            raw.at[chunk(c), pl.ds(pl.multiple_of(own_col + p * bit, LANES), bit)],
+            far_sem.at[c, p], peer(b),
+        )
+
+    def hop(c, b, up, from_own, first=0, width=None):
+        width = ch if width is None else width
+        col = first + (b * ch - (slab_ch - HALO) if up else HALO + slab_ch + b * ch)
         if from_own:
             src = cube.at[pl.ds(pl.multiple_of(own_rows + spans[c][0], 8), spans[c][1]), :]
         else:
-            src = raw.at[chunk(c), pl.ds(HALO + b * ch, ch)]
+            src = raw.at[chunk(c), pl.ds(HALO + b * ch + first, width)]
         to = {"chan": me + group if up else me - group}
-        return remote(src, raw.at[chunk(c), pl.ds(col, ch)], halo_sem.at[c], to)
+        return remote(src, raw.at[chunk(c), pl.ds(col, width)], halo_sem.at[c], to)
 
     def amount(r, width, recv_sem):
         ref = raw.at[r, 0:width]
@@ -200,15 +205,15 @@
                 def _():
                     hop(c, b, False, True).start()
 
-    def pass_on(c, b):
+    def pass_on(c, b, *stretch):
         if goes_up(b):
             @pl.when(slab < slabs - 1)
             def _():
-                hop(c, b, True, False).start()
+                hop(c, b, True, False, *stretch).start()
         if goes_down(b):
             @pl.when(slab > 0)
             def _():
-                hop(c, b, False, False).start()
+                hop(c, b, False, False, *stretch).start()
 
     def forward_near():
         amount(pl.ds(0, rows), ch, near_sem).wait_recv()
@@ -220,22 +225,30 @@
                 def _():
                     pass_on(c, b)
 
-    def forward_far(c):
-        amount(chunk(c), (group - 2) * ch, far_sem.at[c]).wait_recv()
+    def feed(c, p):
         for b in range(group):
             @pl.when(g // 2 != b // 2)
             def _():
-                pass_on(c, b)
+                far_send(c, p, b).start()
+
+    def forward_far(c, p):
+        amount(chunk(c), (group - 2) * bit, far_sem.at[c, p]).wait_recv()
+        for b in range(group):
+            @pl.when(g // 2 != b // 2)
+            def _():
+                pass_on(c, b, p * bit, bit)
+        later = c * pieces + p + WINDOW
+        if later < len(spans) * pieces:
+            feed(later // pieces, later % pieces)
 
     def halo_wait(c):
         if slabs > 1:
             sided(lambda width: amount(chunk(c), width, halo_sem.at[c]).wait_recv())
 
     for c in range(len(spans)):
-        for b in range(group):
-            @pl.when(g // 2 != b // 2)
-            def _():
-                far_send(c, b).start()
+        for p in range(pieces):
+            if c * pieces + p < WINDOW:
+                feed(c, p)
         if c == 0:
             for b in range(group):
                 @pl.when((g != b) & (g // 2 == b // 2))
@@ -354,25 +367,26 @@
         snip(*spans[c])
 
     part = spans[0][1]
-    lanes = lax.broadcasted_iota(jnp.int32, (part, LANES), 1)
-    place = lanes // TERMS
+    place = lax.broadcasted_iota(jnp.int32, (part, LANES), 1) // TERMS
 
     def gather(v):
         for shift in (4 * TERMS, 2 * TERMS, TERMS):
             v = v + pltpu.roll(v, shift, 1)
         return v
 
-    def products(c):
-        whole = fit[chunk(c), :]
+    def products(first, last):
+        tall = (last - first + 1) * part
+        whole = fit[spans[first][0] : spans[first][0] + tall, :]
         hi = whole.astype(BF16).astype(F32)
         lo = whole - hi
         both = jnp.concatenate(
             [hi[:, 0:half], lo[:, 0:half], hi[:, half:], lo[:, half:]], axis=0
         ).astype(BF16)
         rhs = jnp.dot(both, w3[...], preferred_element_type=F32)
-        low = rhs[0:part] + rhs[part : 2 * part]
-        high = rhs[2 * part : 3 * part] + rhs[3 * part :]
-        return jnp.where(lanes < 3 * TERMS, low, high)
+        low = rhs[0:tall] + rhs[tall : 2 * tall]
+        high = rhs[2 * tall : 3 * tall] + rhs[3 * tall :]
+        lane = lax.broadcasted_iota(jnp.int32, (tall, LANES), 1)
+        return jnp.where(lane < 3 * TERMS, low, high)
 
     def send_sums(late):
         mine_at = sums.at[late * n_chan + me]
@@ -390,26 +404,33 @@
     filled = raw.at[:, 0 : (group + 1) * ch]
     for c in range(count + lag):
         if c < count:
-            forward_far(c)
+            forward_far(c, 0)
+        if c == lag:
+            pltpu.make_async_copy(filled, filled, own_sem).wait()
         if c < lag:
             for q in range(c * pairs // lag, (c + 1) * pairs // lag):
                 weigh(q)
-            if c == lag - 1:
-                shape_own()
+        else:
+            process(c - lag)
+        if c < count:
+            for p in range(1, pieces):
+                forward_far(c, p)
         if 2 <= c + 1 < points:
             relay(c + 1)
-        if c == lag:
-            pltpu.make_async_copy(filled, filled, own_sem).wait()
+        if c == lag - 1:
+            shape_own()
         if c >= lag:
             done = c - lag
-            process(done)
-            found = products(done)
-            if done < count - 1:
-                early = jnp.where(place == done, gather(found), early)
+            if done < count - 1 and (count - done) % 2 == 0 and (done > 0 or count < 4):
+                first = 0 if done < 3 else done - 1
+                found = gather(products(first, done))
+                for i in range(first, done + 1):
+                    rows_of = found[(i - first) * part : (i - first + 1) * part]
+                    early = jnp.where(place == i, rows_of, early)
             if done == count - 2:
                 sums[me] = early
                 send_sums(0)
-    sums[n_chan + me] = found
+    sums[n_chan + me] = products(count - 1, count - 1)
     send_sums(1)
 
     sided(lambda width: amount(pl.ds(0, rows), (group - 1) * ch + width, near_sem).wait_send())
@@ -443,16 +464,23 @@
             b * rows,
             jnp.concatenate([jnp.where(place == c, tot, 0.0) for c in range(count - 1)], axis=0),
         )
+    for b in range(group):
+        r = slice(b * rows, b * rows + spans[-1][0])
+        mine[r, :] = mine[r, :] - jnp.dot(
+            left_out[r, :], right_out[...], preferred_element_type=F32
+        )
     sums_wait(0, 2 * (n_chan - 1), sum_recv.at[0]).wait_send()
     sums_wait(0, n_chan - 1, sum_recv.at[1]).wait_recv()
     for b in range(group):
         put_left(b * rows + spans[-1][0], over_slabs(1, b))
 
 
-def subtract(cube, left, right, out, buf, sem):
-    step = max(cube.shape[0] // SPLIT, 16)
-    for start in range(0, cube.shape[0], step):
-        r = pl.ds(start, step)
+def subtract(rows, part, cube, left, right, out, buf, sem):
+    for start in range(0, cube.shape[0], rows):
+        r = pl.ds(start, rows - part)
+        pltpu.make_async_copy(cube.at[r, :], out.at[r, :], sem).start()
+    for start in range(rows - part, cube.shape[0], rows):
+        r = pl.ds(start, part)
         buf[r, :] = cube[r, :] - jnp.dot(left[r, :], right[...], preferred_element_type=F32)
         pltpu.make_async_copy(buf.at[r, :], out.at[r, :], sem).start()
     pltpu.make_async_copy(buf, out, sem).wait()
@@ -495,7 +523,7 @@
             pltpu.VMEM((slab_ch // 2, LANES), BF16),
             pltpu.VMEM((2 * n_chan, part, LANES), F32),
             dma((4,)), dma, pltpu.SemaphoreType.REGULAR((2,)), dma, dma,
-            dma((chunks,)), dma((chunks,)), dma, dma((2,)),
+            dma((chunks, PIECES if ch >= PIECES * LANES else 1)), dma((chunks,)), dma, dma((2,)),
         ],
         compiler_params=pltpu.CompilerParams(
             collective_id=0, has_side_effects=True
@@ -503,7 +531,7 @@
     )(windows, cube, mask.reshape(-1, LANES), mask.reshape(1, total), lin)
     left, right, mine = (pltpu.with_memory_space_constraint(a, pltpu.VMEM) for a in kept)
     return pl.pallas_call(
-        subtract,
+        functools.partial(subtract, rows, part),
         out_shape=jax.ShapeDtypeStruct((pix, ch), F32),
         in_specs=[vmem, vmem, vmem],
         out_specs=hbm,

time: 28.6 us -> 27.6 us (0.965)
  Pallas kernels: 28.5 us -> 27.5 us
    pallas_call x1, Pallas kernels: 27.3 us -> 26.5 us  [per_device(): pl.pallas_call(functools.partial(kernel, n_chan, group, total), out_shape...]
where the time goes in v3:
time: 27.6 us; the launch traced here: 27.5 us
  Pallas kernels  27.5 us (100%)
    pallas_call x1, Pallas kernels, per_device(): pl.pallas_call(functools.partial(kernel, n_chan, group, total), out_shape...  26.5 us
    pallas_call x1, Pallas kernels, per_device(): pl.pallas_call(functools.partial(subtract, rows, part), out_shape=jax.Sha...  0.96 us

profile of v3, /device:TPU:0, one launch (start us, length us, event | category | flops | bytes accessed | tf_op | source)
XLA Modules:
  0.0 27.5 jit_solution(340956117796995926)
XLA Ops:
  0.0 26.5 %shard_map.46 = (bf16[256,128]{1,0:T(8,128)(2,1)S(1)}, bf16[128,1024]{1,0:T(8,128)(2,1)S(1)}, f32[256,1024]{1,0:T(8,128)S(1)}) custom-call(s32[8]{0:T(128)} %windows_hbm.1, f32[256,1024]{1,0:T(8,128)} %cube.1, s32[128,128]{1,0:T(8,128)} %bitcast.2, s32[1,16384]{1,0:T(1,128)} %bitcast.3, f32[31,16,16]{2,1,0:T(8,128)} %constant.2.clone.lin_hbm), custom_call_target="tpu_custom_call" | custom-call | tf_op jit(solution)/shard_map/pallas_call | solution.py:504
  26.5 1.0 %shard_map.47 = f32[256,1024]{1,0:T(8,128)} custom-call(f32[256,1024]{1,0:T(8,128)S(1)} %get-tuple-element.8.cube, bf16[256,128]{1,0:T(8,128)(2,1)S(1)} %get-tuple-element.9.left, bf16[128,1024]{1,0:T(8,128)(2,1)S(1)} %get-tuple-element.10.right), custom_call_target="tpu_custom_call" | custom-call | tf_op jit(solution)/shard_map/pallas_call | solution.py:533

commit v4 on v3

--- a/solution.py
+++ b/solution.py
@@ -18,6 +18,7 @@
 LAG = 3
 AHEAD = 3
 PIECES = 2
+LATE = 3
 WINDOW = 10
 MESH = pl.DeviceIdType.MESH
 F32 = jnp.float32
@@ -62,7 +63,7 @@
     windows_hbm, cube, mask_sq_hbm, mask_row_hbm, lin_hbm,
     left_out, right_out, mine,
     windows, mask_sq, mask_row, lin, raw, ping, pong, fit, table, w3, sums,
-    load_sem, own_sem, token, send_sem, near_sem, far_sem, halo_sem, sum_send, sum_recv,
+    load_sem, own_sem, token, send_sem, last_sem, near_sem, far_sem, halo_sem, sum_send, sum_recv,
 ):
     pix, ch = cube.shape
     rows = raw.shape[0]
@@ -70,6 +71,8 @@
     tiles = slab_ch // LANES
     slabs = n_chan // group
     spans = chunk_spans(rows)
+    last = len(spans) - 2
+    order = [*range(last), last + 1, last]
     pieces = far_sem.shape[1]
     bit = ch // pieces
     me = lax.axis_index("chan")
@@ -147,9 +150,10 @@
     def chunk(c):
         return pl.ds(*spans[c])
 
-    def remote(src, dst, recv_sem, to):
+    def remote(src, dst, recv_sem, to, sent=None):
         return pltpu.make_async_remote_copy(
-            src_ref=src, dst_ref=dst, send_sem=send_sem, recv_sem=recv_sem,
+            src_ref=src, dst_ref=dst, recv_sem=recv_sem,
+            send_sem=send_sem if sent is None else sent,
             device_id=to, device_id_type=MESH,
         )
 
@@ -173,11 +177,46 @@
         else:
             src = raw.at[chunk(c), pl.ds(HALO + b * ch + first, width)]
         to = {"chan": me + group if up else me - group}
-        return remote(src, raw.at[chunk(c), pl.ds(col, width)], halo_sem.at[c], to)
-
-    def amount(r, width, recv_sem):
+        sent = last_sem if c == last else None
+        return remote(src, raw.at[chunk(c), pl.ds(col, width)], halo_sem.at[c], to, sent)
+
+    def amount(r, width, recv_sem, sent=None):
         ref = raw.at[r, 0:width]
-        return remote(ref, ref, recv_sem, {"chan": me})
+        return remote(ref, ref, recv_sem, {"chan": me}, sent)
+
+    def direct(b, up):
+        col = b * ch - (slab_ch - HALO) if up else HALO + slab_ch + b * ch
+        for to in range(group):
+            if to // 2 != b // 2:
+                remote(
+                    cube.at[pl.ds(to * rows + spans[last][0], spans[last][1]), :],
+                    raw.at[chunk(last), pl.ds(col, ch)], halo_sem.at[last],
+                    {"chan": (slab + (1 if up else -1)) * group + to}, last_sem,
+                ).start()
+
+    def direct_all():
+        for b in range(group):
+            if goes_up(b):
+                @pl.when((g == b) & (slab < slabs - 1))
+                def _():
+                    direct(b, True)
+            if goes_down(b):
+                @pl.when((g == b) & (slab > 0))
+                def _():
+                    direct(b, False)
+
+    def direct_wait():
+        for b in range(group):
+            beside = [a for a in range(group) if a // 2 == b // 2]
+            up = sum(map(goes_up, beside)) + (group - 2) * goes_up(b)
+            down = sum(map(goes_down, beside)) + (group - 2) * goes_down(b)
+            for blocks, where in (
+                (up + down, inner), (up, slab == 0), (down, slab == slabs - 1)
+            ):
+                if blocks and slabs > 1:
+                    @pl.when((g == b) & where)
+                    def _():
+                        amount(chunk(last), blocks * ch, near_sem, last_sem).wait_send()
 
     inner = (slab > 0) & (slab < slabs - 1)
 
@@ -231,15 +270,19 @@
             def _():
                 far_send(c, p, b).start()
 
-    def forward_far(c, p):
+    def forward_far(turn, p):
+        c = order[turn]
         amount(chunk(c), (group - 2) * bit, far_sem.at[c, p]).wait_recv()
         for b in range(group):
+            if c == last:
+                break
+
             @pl.when(g // 2 != b // 2)
             def _():
                 pass_on(c, b, p * bit, bit)
-        later = c * pieces + p + WINDOW
+        later = turn * pieces + p + WINDOW
         if later < len(spans) * pieces:
-            feed(later // pieces, later % pieces)
+            feed(order[later // pieces], later % pieces)
 
     def halo_wait(c):
         if slabs > 1:
@@ -248,7 +291,7 @@
     for c in range(len(spans)):
         for p in range(pieces):
             if c * pieces + p < WINDOW:
-                feed(c, p)
+                feed(order[c], p)
         if c == 0:
             for b in range(group):
                 @pl.when((g != b) & (g // 2 == b // 2))
@@ -389,7 +432,7 @@
         return jnp.where(lane < 3 * TERMS, low, high)
 
     def send_sums(late):
-        mine_at = sums.at[late * n_chan + me]
+        mine_at = sums.at[pl.ds(n_chan + 2 * me, 2) if late else pl.ds(me, 1)]
         for k in range(1, n_chan):
             pltpu.make_async_remote_copy(
                 src_ref=mine_at, dst_ref=mine_at,
@@ -417,6 +460,8 @@
                 forward_far(c, p)
         if 2 <= c + 1 < points:
             relay(c + 1)
+        if c + 2 == max(points, 3):
+            direct_all()
         if c == lag - 1:
             shape_own()
         if c >= lag:
@@ -427,13 +472,22 @@
                 for i in range(first, done + 1):
                     rows_of = found[(i - first) * part : (i - first + 1) * part]
                     early = jnp.where(place == i, rows_of, early)
-            if done == count - 2:
+            if done == count - LATE - 1:
                 sums[me] = early
                 send_sums(0)
-    sums[n_chan + me] = products(count - 1, count - 1)
+            if done == count - 2:
+                sums[n_chan + 2 * me] = early
+    sums[n_chan + 2 * me + 1] = products(count - 1, count - 1)
     send_sums(1)
 
-    sided(lambda width: amount(pl.ds(0, rows), (group - 1) * ch + width, near_sem).wait_send())
+    share = rows - spans[last][1]
+
+    def sent_wait(width):
+        amount(pl.ds(0, rows), (group - 1) * ch, near_sem).wait_send()
+        amount(pl.ds(0, share), width, near_sem).wait_send()
+
+    sided(sent_wait)
+    direct_wait()
 
     def sums_wait(first, blocks, recv):
         ref = sums.at[first : first + blocks]
@@ -451,28 +505,33 @@
         picked = jnp.where((spot < 2) | (spot == 3), hi, picked)
         left_out[start : start + spread.shape[0], :] = picked.astype(BF16)
 
-    def over_slabs(late, b):
-        tot = sums[late * n_chan + b]
+    def over_slabs(start, stride, b):
+        tot = sums[start + stride * b]
         for z in range(1, slabs):
-            tot = tot + sums[late * n_chan + z * group + b]
+            tot = tot + sums[start + stride * (z * group + b)]
         return tot
 
+    def apart(tot, first, end):
+        return [jnp.where(place == c, tot, 0.0) for c in range(first, end)]
+
+    begun = spans[count - LATE][0]
     sums_wait(0, n_chan - 1, sum_recv.at[0]).wait_recv()
     for b in range(group):
-        tot = over_slabs(0, b)
         put_left(
             b * rows,
-            jnp.concatenate([jnp.where(place == c, tot, 0.0) for c in range(count - 1)], axis=0),
+            jnp.concatenate(apart(over_slabs(0, 1, b), 0, count - LATE), axis=0),
         )
     for b in range(group):
-        r = slice(b * rows, b * rows + spans[-1][0])
+        r = slice(b * rows, b * rows + begun)
         mine[r, :] = mine[r, :] - jnp.dot(
             left_out[r, :], right_out[...], preferred_element_type=F32
         )
-    sums_wait(0, 2 * (n_chan - 1), sum_recv.at[0]).wait_send()
-    sums_wait(0, n_chan - 1, sum_recv.at[1]).wait_recv()
+    sums_wait(0, 3 * (n_chan - 1), sum_recv.at[0]).wait_send()
+    sums_wait(0, 2 * (n_chan - 1), sum_recv.at[1]).wait_recv()
     for b in range(group):
-        put_left(b * rows + spans[-1][0], over_slabs(1, b))
+        mid = apart(over_slabs(n_chan, 2, b), count - LATE, count - 1)
+        end = over_slabs(n_chan + 1, 2, b)
+        put_left(b * rows + begun, jnp.concatenate([*mid, end], axis=0))
 
 
 def subtract(rows, part, cube, left, right, out, buf, sem):
@@ -521,8 +580,8 @@
             pltpu.VMEM((rows, slab_ch), F32),
             pltpu.VMEM((TERMS, slab_ch), F32),
             pltpu.VMEM((slab_ch // 2, LANES), BF16),
-            pltpu.VMEM((2 * n_chan, part, LANES), F32),
-            dma((4,)), dma, pltpu.SemaphoreType.REGULAR((2,)), dma, dma,
+            pltpu.VMEM((3 * n_chan, part, LANES), F32),
+            dma((4,)), dma, pltpu.SemaphoreType.REGULAR((2,)), dma, dma, dma,
             dma((chunks, PIECES if ch >= PIECES * LANES else 1)), dma((chunks,)), dma, dma((2,)),
         ],
         compiler_params=pltpu.CompilerParams(
@@ -531,7 +590,7 @@
     )(windows, cube, mask.reshape(-1, LANES), mask.reshape(1, total), lin)
     left, right, mine = (pltpu.with_memory_space_constraint(a, pltpu.VMEM) for a in kept)
     return pl.pallas_call(
-        functools.partial(subtract, rows, part),
+        functools.partial(subtract, rows, LATE * part),
         out_shape=jax.ShapeDtypeStruct((pix, ch), F32),
         in_specs=[vmem, vmem, vmem],
         out_specs=hbm,

time: 27.6 us -> 27.6 us (level)
  no operation moved by 1% of the time
where the time goes in v4:
time: 27.6 us; the launch traced here: 27.4 us
  Pallas kernels  27.4 us (99%)
    pallas_call x1, Pallas kernels, per_device(): pl.pallas_call(functools.partial(kernel, n_chan, group, total), out_shape...  26.4 us
    pallas_call x1, Pallas kernels, per_device(): pl.pallas_call(functools.partial(subtract, rows, LATE * part), out_shape=...  0.96 us

profile of v4, /device:TPU:0, one launch (start us, length us, event | category | flops | bytes accessed | tf_op | source)
XLA Modules:
  0.0 27.4 jit_solution(1380998962844231878)
XLA Ops:
  0.0 26.4 %shard_map.46 = (bf16[256,128]{1,0:T(8,128)(2,1)S(1)}, bf16[128,1024]{1,0:T(8,128)(2,1)S(1)}, f32[256,1024]{1,0:T(8,128)S(1)}) custom-call(s32[8]{0:T(128)} %windows_hbm.1, f32[256,1024]{1,0:T(8,128)} %cube.1, s32[128,128]{1,0:T(8,128)} %bitcast.2, s32[1,16384]{1,0:T(1,128)} %bitcast.3, f32[31,16,16]{2,1,0:T(8,128)} %constant.2.clone.lin_hbm), custom_call_target="tpu_custom_call" | custom-call | tf_op jit(solution)/shard_map/pallas_call | solution.py:563
  26.4 1.0 %shard_map.47 = f32[256,1024]{1,0:T(8,128)} custom-call(f32[256,1024]{1,0:T(8,128)S(1)} %get-tuple-element.8.cube, bf16[256,128]{1,0:T(8,128)(2,1)S(1)} %get-tuple-element.9.left, bf16[128,1024]{1,0:T(8,128)(2,1)S(1)} %get-tuple-element.10.right), custom_call_target="tpu_custom_call" | custom-call | tf_op jit(solution)/shard_map/pallas_call | solution.py:592

commit v5 on v4

--- a/solution.py
+++ b/solution.py
@@ -432,7 +432,7 @@
         return jnp.where(lane < 3 * TERMS, low, high)
 
     def send_sums(late):
-        mine_at = sums.at[pl.ds(n_chan + 2 * me, 2) if late else pl.ds(me, 1)]
+        mine_at = sums.at[late * n_chan + me]
         for k in range(1, n_chan):
             pltpu.make_async_remote_copy(
                 src_ref=mine_at, dst_ref=mine_at,
@@ -444,6 +444,10 @@
     lag = min(LAG, count)
     pairs = half // step
     early = jnp.zeros((part, LANES), F32)
+
+    def spot_of(c):
+        return c if c < count - LATE else c - (count - LATE) + 6
+
     filled = raw.at[:, 0 : (group + 1) * ch]
     for c in range(count + lag):
         if c < count:
@@ -471,13 +475,12 @@
                 found = gather(products(first, done))
                 for i in range(first, done + 1):
                     rows_of = found[(i - first) * part : (i - first + 1) * part]
-                    early = jnp.where(place == i, rows_of, early)
+                    early = jnp.where(place == spot_of(i), rows_of, early)
             if done == count - LATE - 1:
                 sums[me] = early
                 send_sums(0)
-            if done == count - 2:
-                sums[n_chan + 2 * me] = early
-    sums[n_chan + 2 * me + 1] = products(count - 1, count - 1)
+    found = products(count - 1, count - 1)
+    sums[n_chan + me] = jnp.where(place < 6, found, early)
     send_sums(1)
 
     share = rows - spans[last][1]
@@ -505,32 +508,33 @@
         picked = jnp.where((spot < 2) | (spot == 3), hi, picked)
         left_out[start : start + spread.shape[0], :] = picked.astype(BF16)
 
-    def over_slabs(start, stride, b):
-        tot = sums[start + stride * b]
+    def over_slabs(late, b):
+        tot = sums[late * n_chan + b]
         for z in range(1, slabs):
-            tot = tot + sums[start + stride * (z * group + b)]
+            tot = tot + sums[late * n_chan + z * group + b]
         return tot
 
     def apart(tot, first, end):
-        return [jnp.where(place == c, tot, 0.0) for c in range(first, end)]
+        return [jnp.where(place == spot_of(c), tot, 0.0) for c in range(first, end)]
 
     begun = spans[count - LATE][0]
     sums_wait(0, n_chan - 1, sum_recv.at[0]).wait_recv()
     for b in range(group):
         put_left(
             b * rows,
-            jnp.concatenate(apart(over_slabs(0, 1, b), 0, count - LATE), axis=0),
+            jnp.concatenate(apart(over_slabs(0, b), 0, count - LATE), axis=0),
         )
     for b in range(group):
         r = slice(b * rows, b * rows + begun)
         mine[r, :] = mine[r, :] - jnp.dot(
             left_out[r, :], right_out[...], preferred_element_type=F32
         )
-    sums_wait(0, 3 * (n_chan - 1), sum_recv.at[0]).wait_send()
-    sums_wait(0, 2 * (n_chan - 1), sum_recv.at[1]).wait_recv()
+    sums_wait(0, 2 * (n_chan - 1), sum_recv.at[0]).wait_send()
+    sums_wait(0, n_chan - 1, sum_recv.at[1]).wait_recv()
     for b in range(group):
-        mid = apart(over_slabs(n_chan, 2, b), count - LATE, count - 1)
-        end = over_slabs(n_chan + 1, 2, b)
+        tot = over_slabs(1, b)
+        mid = apart(tot, count - LATE, count - 1)
+        end = jnp.where(place < 6, tot, 0.0)
         put_left(b * rows + begun, jnp.concatenate([*mid, end], axis=0))
 
 
@@ -580,7 +584,7 @@
             pltpu.VMEM((rows, slab_ch), F32),
             pltpu.VMEM((TERMS, slab_ch), F32),
             pltpu.VMEM((slab_ch // 2, LANES), BF16),
-            pltpu.VMEM((3 * n_chan, part, LANES), F32),
+            pltpu.VMEM((2 * n_chan, part, LANES), F32),
             dma((4,)), dma, pltpu.SemaphoreType.REGULAR((2,)), dma, dma, dma,
             dma((chunks, PIECES if ch >= PIECES * LANES else 1)), dma((chunks,)), dma, dma((2,)),
         ],

time: 27.6 us -> 26.7 us (0.967)
  Pallas kernels: 27.4 us -> 26.5 us
    pallas_call x1, Pallas kernels: 26.4 us -> 25.6 us  [per_device(): pl.pallas_call(functools.partial(kernel, n_chan, group, total), out_shape...]
where the time goes in v5:
time: 26.7 us; the launch traced here: 26.5 us
  Pallas kernels  26.5 us (99%)
    pallas_call x1, Pallas kernels, per_device(): pl.pallas_call(functools.partial(kernel, n_chan, group, total), out_shape...  25.6 us
    pallas_call x1, Pallas kernels, per_device(): pl.pallas_call(functools.partial(subtract, rows, LATE * part), out_shape=...  0.96 us

profile of v5, /device:TPU:0, one launch (start us, length us, event | category | flops | bytes accessed | tf_op | source)
XLA Modules:
  0.0 26.5 jit_solution(2107420237353814922)
XLA Ops:
  0.0 25.6 %shard_map.46 = (bf16[256,128]{1,0:T(8,128)(2,1)S(1)}, bf16[128,1024]{1,0:T(8,128)(2,1)S(1)}, f32[256,1024]{1,0:T(8,128)S(1)}) custom-call(s32[8]{0:T(128)} %windows_hbm.1, f32[256,1024]{1,0:T(8,128)} %cube.1, s32[128,128]{1,0:T(8,128)} %bitcast.2, s32[1,16384]{1,0:T(1,128)} %bitcast.3, f32[31,16,16]{2,1,0:T(8,128)} %constant.2.clone.lin_hbm), custom_call_target="tpu_custom_call" | custom-call | tf_op jit(solution)/shard_map/pallas_call | solution.py:567
  25.6 1.0 %shard_map.47 = f32[256,1024]{1,0:T(8,128)} custom-call(f32[256,1024]{1,0:T(8,128)S(1)} %get-tuple-element.8.cube, bf16[256,128]{1,0:T(8,128)(2,1)S(1)} %get-tuple-element.9.left, bf16[128,1024]{1,0:T(8,128)(2,1)S(1)} %get-tuple-element.10.right), custom_call_target="tpu_custom_call" | custom-call | tf_op jit(solution)/shard_map/pallas_call | solution.py:596

commit v6 on v5

--- a/solution.py
+++ b/solution.py
@@ -470,7 +470,7 @@
             shape_own()
         if c >= lag:
             done = c - lag
-            if done < count - 1 and (count - done) % 2 == 0 and (done > 0 or count < 4):
+            if done < count - LATE and (count - done) % 2 == 0 and (done > 0 or count < 4):
                 first = 0 if done < 3 else done - 1
                 found = gather(products(first, done))
                 for i in range(first, done + 1):
@@ -479,8 +479,12 @@
             if done == count - LATE - 1:
                 sums[me] = early
                 send_sums(0)
-    found = products(count - 1, count - 1)
-    sums[n_chan + me] = jnp.where(place < 6, found, early)
+    found = products(count - LATE, count - 1)
+    done = gather(found[: (LATE - 1) * part])
+    tile = jnp.where(place < 6, found[(LATE - 1) * part :], 0.0)
+    for i in range(LATE - 1):
+        tile = jnp.where(place == 6 + i, done[i * part : (i + 1) * part], tile)
+    sums[n_chan + me] = tile
     send_sums(1)
 
     share = rows - spans[last][1]

time: 26.7 us -> 26.6 us (level)
  no operation moved by 1% of the time
where the time goes in v6:
time: 26.6 us; the launch traced here: 26.4 us
  Pallas kernels  26.4 us (99%)
    pallas_call x1, Pallas kernels, per_device(): pl.pallas_call(functools.partial(kernel, n_chan, group, total), out_shape...  25.5 us
    pallas_call x1, Pallas kernels, per_device(): pl.pallas_call(functools.partial(subtract, rows, LATE * part), out_shape=...  0.96 us

profile of v6, /device:TPU:0, one launch (start us, length us, event | category | flops | bytes accessed | tf_op | source)
XLA Modules:
  0.0 26.4 jit_solution(8742499047704115120)
XLA Ops:
  0.0 25.5 %shard_map.46 = (bf16[256,128]{1,0:T(8,128)(2,1)S(1)}, bf16[128,1024]{1,0:T(8,128)(2,1)S(1)}, f32[256,1024]{1,0:T(8,128)S(1)}) custom-call(s32[8]{0:T(128)} %windows_hbm.1, f32[256,1024]{1,0:T(8,128)} %cube.1, s32[128,128]{1,0:T(8,128)} %bitcast.2, s32[1,16384]{1,0:T(1,128)} %bitcast.3, f32[31,16,16]{2,1,0:T(8,128)} %constant.2.clone.lin_hbm), custom_call_target="tpu_custom_call" | custom-call | tf_op jit(solution)/shard_map/pallas_call | solution.py:571
  25.5 1.0 %shard_map.47 = f32[256,1024]{1,0:T(8,128)} custom-call(f32[256,1024]{1,0:T(8,128)S(1)} %get-tuple-element.8.cube, bf16[256,128]{1,0:T(8,128)(2,1)S(1)} %get-tuple-element.9.left, bf16[128,1024]{1,0:T(8,128)(2,1)S(1)} %get-tuple-element.10.right), custom_call_target="tpu_custom_call" | custom-call | tf_op jit(solution)/shard_map/pallas_call | solution.py:600
